TPU v7x, 1024 devices: a whole 4x4x32 slice. The times are simulated.
1024 devices in a mesh: lat: 16 (over y, x), lev: 64 (over z, core).
Axes of the slice: x: 4, y: 4, z: 32, core: 2. Of those that a mesh axis runs over, the one named last changes fastest.
Arguments:
- adjoint_grid: bfloat16 [128, 768, 1536], P('lev', 'lat'), may hold values from -6 to 6
- wind: bfloat16 [128, 768, 1536], P('lev', 'lat'), may hold values from -6 to 6
- legendre: bfloat16 [1024, 768, 576], P(('lat', 'lev')), may hold values from -0.21875 to 0.21875
- vertical: bfloat16 [16, 128, 128], replicated, may hold values from -0.5 to 0.5
- pair_table: int32 [256], replicated, may hold values from 0 to 255, each once
- degree_matrix: int32 [512], replicated, may hold values from 0 to 15
Outputs:
- adjoint_out: bfloat16 [128, 768, 1536], P('lev', 'lat')
Inputs may be any that keep to these rules, and one draw needn't show every extreme that they name: `pair_table`: the values are distinct: every pair (m, 511 - m) with m < 256 stands in exactly one slot.
All inputs are finite; a program needn't handle non-finite values.
Results may differ from a plain program's by a relative error of at most 0.008.
Values may be sent and summed in bfloat16 or wider, within the bound.
A program may use at most 64 MiB of HBM per device.

v0:
```python
import math

import jax
import jax.numpy as jnp
from jax import lax
from jax.sharding import PartitionSpec as P

N = 512


def fourier_basis(wavenumbers, points):
    longitude = jnp.arange(points, dtype=jnp.int32)
    phases = wavenumbers[:, :, None] * longitude[None, None, :] % points
    angles = phases.astype(jnp.float32) * (2.0 * jnp.pi / points)
    basis = jnp.stack([jnp.cos(angles), -jnp.sin(angles)], axis=2)
    return basis.reshape(-1, points)


def member_layout(lower_wave, row_total):
    packed_buffer = jnp.arange(row_total, dtype=jnp.int32)
    first_member = packed_buffer[None, :] < (N - lower_wave)[:, None]
    second_member = jnp.logical_not(first_member) & (packed_buffer[None, :] <= N)
    degree = jnp.where(
        first_member, lower_wave[:, None] + packed_buffer[None, :], packed_buffer[None, :] - 1
    )
    degree = jnp.clip(degree, 0, N - 1)
    return (first_member, second_member, degree)


def solve_columns(spectral_state, matrix_index, vertical):

    def add_matrix(operator_index, running):
        product = jnp.einsum(
            "xjm,mg->xjg",
            spectral_state,
            vertical[operator_index],
            preferred_element_type=jnp.float32,
        )
        return running + jnp.where((matrix_index == operator_index)[:, :, None], product, 0.0)

    zero_sums = jnp.zeros(spectral_state.shape, jnp.float32)
    return lax.fori_loop(0, vertical.shape[0], add_matrix, zero_sums).astype(jnp.bfloat16)


def body(adjoint_grid, wind, legendre, vertical, pair_table, degree_matrix):
    vertical_level_rows, lat_rows, points = adjoint_grid.shape
    lat_devices = lax.axis_size("lat")
    lev_devices = lax.axis_size("lev")
    slots = legendre.shape[0]
    all_lats = legendre.shape[1]
    packed_rows = legendre.shape[2]
    levels = vertical.shape[1]
    wavenumbers = jnp.stack([pair_table, N - 1 - pair_table], axis=1)
    basis = fourier_basis(wavenumbers, points)
    analysis_table = (basis * (1.0 / math.sqrt(points))).astype(jnp.bfloat16)
    synthesis_table = (basis * (1.0 / math.sqrt(N))).astype(jnp.bfloat16)
    fourier = jnp.einsum(
        "cx,vlx->cvl", analysis_table, adjoint_grid, preferred_element_type=jnp.float32
    )
    fourier = fourier.astype(jnp.bfloat16).reshape(
        lat_devices, lev_devices, slots, vertical_level_rows, lat_rows
    )
    moved = lax.all_to_all(
        lax.all_to_all(fourier, "lat", split_axis=0, concat_axis=4, tiled=True),
        "lev",
        split_axis=1,
        concat_axis=3,
        tiled=True,
    )
    field_stack = moved.reshape(slots, levels, all_lats)
    first_slot = (lax.axis_index("lat") * lev_devices + lax.axis_index("lev")) * slots
    column = first_slot + jnp.arange(slots, dtype=jnp.int32)
    lower_cols = jnp.take(pair_table, column // 4)
    member = column // 2 % 2
    first_member, second_member, degree = member_layout(lower_cols, packed_rows)
    own_rows = jnp.where((member == 0)[:, None], first_member, second_member).astype(jnp.float32)
    spectral_state = jnp.einsum(
        "peq,pae->pqa", legendre, field_stack, preferred_element_type=jnp.float32
    )
    spectral_state = (spectral_state * own_rows[:, :, None]).astype(jnp.bfloat16)
    matrix_index = jnp.take(degree_matrix, degree)
    solved_columns = solve_columns(spectral_state, matrix_index, vertical)
    gridpoint_coefficients = jnp.einsum(
        "ncb,nba->nac", legendre, solved_columns, preferred_element_type=jnp.float32
    )
    gridpoint_coefficients = gridpoint_coefficients.astype(jnp.bfloat16).reshape(
        1, 1, slots, levels, all_lats
    )
    returned = lax.all_to_all(
        lax.all_to_all(gridpoint_coefficients, "lat", split_axis=4, concat_axis=0, tiled=True),
        "lev",
        split_axis=3,
        concat_axis=1,
        tiled=True,
    )
    columns = returned.reshape(lat_devices * lev_devices * slots, vertical_level_rows, lat_rows)
    regridded = jnp.einsum(
        "cvl,cx->vlx", columns, synthesis_table, preferred_element_type=jnp.float32
    )
    return (regridded * wind.astype(jnp.float32)).astype(jnp.bfloat16)


def solution(mesh):
    placed = (
        P("lev", "lat", None),
        P("lev", "lat", None),
        P(("lat", "lev"), None, None),
        P(),
        P(),
        P(),
    )
    return jax.shard_map(
        body, mesh=mesh, in_specs=placed, out_specs=P("lev", "lat", None), check_vma=False
    )
```

profile of v0, /device:TPU:1, one launch (start us, length us, event | category | flops | bytes accessed | tf_op | source)
XLA Modules:
  0.0 197.4 jit_solution(3442890102843857139)
XLA Ops:
  1.4 13.1 %fusion.10 = (f32[256,2,1,1536]{3,0,2,1:T(8,128)S(1)}, f32[256,2,1,1536]{3,0,2,1:T(8,128)S(1)}) fusion(s32[256,2]{0,1:T(2,128)S(1)} %pad_add_fusion), kind=kLoop, calls=%fused_computation.19 | loop fusion | flops 7864320 | bytes 6293504 | tf_op jit(solution)/shard_map/cos | solution.py:15
  14.5 2.4 %multiply_convert_fusion.1 = (bf16[256,2,2,1536]{3,0,2,1:T(8,128)(2,1)S(1)}, bf16[256,2,2,1536]{3,0,2,1:T(8,128)(2,1)}) fusion(f32[256,2,1,1536]{3,0,2,1:T(8,128)S(1)} %get-tuple-element.142, f32[256,2,1,1536]{3,0,2,1:T(8,128)S(1)} %get-tuple-element.141), kind=kLoop, calls=%fused_computation.11 | loop fusion | flops 7864320 | bytes 12582912 | tf_op jit(solution)/shard_map/convert_element_type | solution.py:55
  16.9 4.9 %copy.33 = bf16[256,2,2,1536]{3,2,1,0:T(2,128)(2,1)} copy(bf16[256,2,2,1536]{3,0,2,1:T(8,128)(2,1)S(1)} %get-tuple-element.139) | data formatting | bytes 6291456 | tf_op jit(solution)/shard_map/convert_element_type | solution.py:55
  21.8 7.6 %reshape.296 = bf16[1024,1536,1]{1,0,2:T(8,128)(2,1)} reshape(bf16[256,2,2,1536]{3,2,1,0:T(2,128)(2,1)} %copy.33) | data formatting | bytes 6291456 | tf_op jit(solution)/shard_map/convert_element_type | solution.py:55
  29.4 3.0 %convolution_convert_fusion = bf16[1024,2,48]{0,2,1:T(8,128)(2,1)S(1)} fusion(bf16[1024,1536,1]{1,0,2:T(8,128)(2,1)} %reshape.296, bf16[2,48,1536]{2,1,0:T(8,128)(2,1)S(1)} %copy-done.4), kind=kOutput, calls=%fused_computation.23 | convolution fusion | flops 302088192 | bytes 3637248 | tf_op jit(solution)/shard_map/cx,vlx->cvl/dot_general | solution.py:57
  33.0 14.6 %all_to_all.54 = bf16[16,2,3072]{2,1,0:T(2,128)(2,1)S(1)} all-to-all(bf16[16,2,3072]{2,1,0:T(2,128)(2,1)S(1)} %reshape.304), channel_id=1, replica_groups=mesh['lat'=16,'lev'=64] {'lat'}, dimensions={0} | all-to-all | bytes 393216 | tf_op jit(solution)/shard_map/all_to_all | solution.py:64
  48.6 1.4 reshape.299
  50.0 31.0 %all-to-all-start.1 = ((bf16[1,64,1,2,768]{4,3,2,0,1:T(2,128)(2,1)}), bf16[1,64,1,2,768]{4,3,2,0,1:T(2,128)(2,1)S(1)}, u32[]{:S(2)}, u32[]{:S(2)}) async-start(bf16[1,64,1,2,768]{4,3,2,0,1:T(2,128)(2,1)} %reshape.299), calls=%async_computation.1 | async-start | bytes 393216 | tf_op jit(solution)/shard_map/all_to_all | solution.py:63
  82.5 4.0 %gather_fusion = s32[576]{0:T(1024)S(1)} fusion(s32[512]{0:T(512)S(1)} %copy-done.1, s32[1024]{0:T(1024)S(1)} %pad_clamp_fusion), kind=kCustom, calls=%fused_computation | custom fusion | bytes 6912 | tf_op jit(solution)/shard_map/jit(_take)/gather | solution.py:81
  86.5 31.0 %all-to-all-done.1 = bf16[1,64,1,2,768]{4,3,2,0,1:T(2,128)(2,1)S(1)} async-done(((bf16[1,64,1,2,768]{4,3,2,0,1:T(2,128)(2,1)}), bf16[1,64,1,2,768]{4,3,2,0,1:T(2,128)(2,1)S(1)}, u32[]{:S(2)}, u32[]{:S(2)}) %all-to-all-start.1) | async-done | bytes 196640 | tf_op jit(solution)/shard_map/all_to_all | solution.py:63
  118.0 16.3 %while.15 = (s32[]{:T(128)}, f32[1,576,128]{2,1,0:T(8,128)S(1)}, s32[1,576]{1,0:T(1,128)S(1)}, bf16[16,128,128]{2,1,0:T(8,128)(2,1)}, bf16[1,576,128]{2,1,0:T(8,128)(2,1)S(1)}, /*index=5*/s32[]{:T(128)}, s32[]{:T(128)}) while((s32[]{:T(128)}, f32[1,576,128]{2,1,0:T(8,128)S(1)}, s32[1,576]{1,0:T(1,128)S(1)}, ...), condition=%wide.region_1.2_spmd.clone, body=%wide.region_0.1_spmd.clone.sunk | while | flops 19096132 | bytes 773607 | solution.py:42
  121.1 1.0 fusion.37
  122.1 1.0 fusion.37
  126.2 1.0 fusion.37
  127.2 1.0 fusion.37
  132.3 1.0 fusion.37
  135.6 1.8 reduce.4
  137.5 9.9 %all_to_all.55 = bf16[16,2,3072]{2,1,0:T(2,128)(2,1)S(1)} all-to-all(bf16[16,2,3072]{2,1,0:T(2,128)(2,1)S(1)} %reshape.306), channel_id=1, replica_groups=mesh['lat'=16,'lev'=64] {'lat'}, dimensions={0} | all-to-all | bytes 393216 | tf_op jit(solution)/shard_map/all_to_all | solution.py:90
  148.0 1.4 reshape.308
  149.4 7.1 %all-to-all-start.3 = ((bf16[64,2,768]{2,1,0:T(2,128)(2,1)}), bf16[64,2,768]{2,1,0:T(2,128)(2,1)S(1)}, u32[]{:S(2)}, u32[]{:S(2)}) async-start(bf16[64,2,768]{2,1,0:T(2,128)(2,1)} %reshape.308), calls=%async_computation.3 | async-start | bytes 393216 | tf_op jit(solution)/shard_map/all_to_all | solution.py:89
  156.5 6.8 %copy.40 = bf16[256,2,2,1536]{3,2,1,0:T(2,128)(2,1)} copy(bf16[256,2,2,1536]{3,0,2,1:T(8,128)(2,1)} %get-tuple-element.140) | data formatting | bytes 6291456 | tf_op jit(solution)/shard_map/convert_element_type | solution.py:56
  163.3 7.6 %reshape.297 = bf16[1024,1536,1]{1,0,2:T(8,128)(2,1)} reshape(bf16[256,2,2,1536]{3,2,1,0:T(2,128)(2,1)} %copy.40) | data formatting | bytes 6291456 | tf_op jit(solution)/shard_map/convert_element_type | solution.py:56
  170.9 22.6 %all-to-all-done.3 = bf16[64,2,768]{2,1,0:T(2,128)(2,1)S(1)} async-done(((bf16[64,2,768]{2,1,0:T(2,128)(2,1)}), bf16[64,2,768]{2,1,0:T(2,128)(2,1)S(1)}, u32[]{:S(2)}, u32[]{:S(2)}) %all-to-all-start.3) | async-done | bytes 196640 | tf_op jit(solution)/shard_map/all_to_all | solution.py:89
  194.1 3.3 %fusion.12 = bf16[2,48,1536]{2,1,0:T(8,128)(2,1)} fusion(bf16[1024,1536,1]{1,0,2:T(8,128)(2,1)} %reshape.297, bf16[2,48,1536]{2,1,0:T(8,128)(2,1)S(1)} %copy-done.2, bf16[1024,2,48]{2,1,0:T(2,128)(2,1)S(1)} %bitcast.70), kind=kOutput, calls=%fused_computation.22 | convolution fusion | flops 302432256 | bytes 3932160 | tf_op jit(solution)/shard_map/cvl,cx->vlx/dot_general | solution.py:97
  (62 shorter events, 17.9 us)
Async XLA Ops:
  0.0 117.6 %copy-start = (bf16[1,768,576]{1,2,0:T(8,128)(2,1)S(1)}, bf16[1,768,576]{1,2,0:T(8,128)(2,1)}, u32[]{:S(2)}) copy-start(bf16[1,768,576]{1,2,0:T(8,128)(2,1)} %param.10) | copy-start | bytes 2654212
  21.8 7.6 %copy-start.4 = (bf16[2,48,1536]{2,1,0:T(8,128)(2,1)S(1)}, bf16[2,48,1536]{2,1,0:T(8,128)(2,1)}, u32[]{:S(2)}) copy-start(bf16[2,48,1536]{2,1,0:T(8,128)(2,1)} %param.8) | copy-start | bytes 884740
  32.3 48.8 %copy-start.3 = (s32[256]{0:T(256)S(1)}, s32[256]{0:T(256)}, u32[]{:S(2)}) copy-start(s32[256]{0:T(256)} %param.12) | copy-start | bytes 3076
  32.3 50.2 %copy-start.1 = (s32[512]{0:T(512)S(1)}, s32[512]{0:T(512)}, u32[]{:S(2)}) copy-start(s32[512]{0:T(512)} %param.13) | copy-start | bytes 6148
  50.0 67.5 %all-to-all-start.1 = ((bf16[1,64,1,2,768]{4,3,2,0,1:T(2,128)(2,1)}), bf16[1,64,1,2,768]{4,3,2,0,1:T(2,128)(2,1)S(1)}, u32[]{:S(2)}, u32[]{:S(2)}) async-start(bf16[1,64,1,2,768]{4,3,2,0,1:T(2,128)(2,1)} %reshape.299), calls=%async_computation.1 | async-start | bytes 393216 | tf_op jit(solution)/shard_map/all_to_all | solution.py:63
  149.4 44.0 %all-to-all-start.3 = ((bf16[64,2,768]{2,1,0:T(2,128)(2,1)}), bf16[64,2,768]{2,1,0:T(2,128)(2,1)S(1)}, u32[]{:S(2)}, u32[]{:S(2)}) async-start(bf16[64,2,768]{2,1,0:T(2,128)(2,1)} %reshape.308), calls=%async_computation.3 | async-start | bytes 393216 | tf_op jit(solution)/shard_map/all_to_all | solution.py:89
  163.3 30.8 %copy-start.2 = (bf16[2,48,1536]{2,1,0:T(8,128)(2,1)S(1)}, bf16[2,48,1536]{2,1,0:T(8,128)(2,1)}, u32[]{:S(2)}) copy-start(bf16[2,48,1536]{2,1,0:T(8,128)(2,1)} %param.9) | copy-start | bytes 884740
where the time goes:
time: 199 us; the launch traced here: 197 us
  waiting for transfers between devices  53.6 us (27%)
  local copies, waits for them, and re-layouts  38.2 us (19%)
  starting transfers between devices  38.1 us (19%)
  blocking collectives  24.5 us (12%)
  matrix products  22.5 us (11%)
  other arithmetic  19.1 us (10%)
    all_to_all x1, waiting for transfers between devices, body(): lax.all_to_all(lax.all_to_all(fourier, 'lat', split_axis=0, concat_axis=4...  31 us
    all_to_all x1, starting transfers between devices, body(): lax.all_to_all(lax.all_to_all(fourier, 'lat', split_axis=0, concat_axis=4...  31 us
    all_to_all x1, waiting for transfers between devices, body(): lax.all_to_all(lax.all_to_all(gridpoint_coefficients, 'lat', split_axis=4...  22.6 us
    dot_general x16, matrix products, add_matrix(): jnp.einsum('xjm,mg->xjg', spectral_state, vertical[operator_index], prefe...  15.5 us
    all_to_all x1, blocking collectives, body(): lax.all_to_all(fourier, 'lat', split_axis=0, concat_axis=4, tiled=True)  14.6 us
    convert_element_type x2, local copies, waits for them, and re-layouts, body(): synthesis_table = (basis * (1.0 / math.sqrt(N))).astype(jnp.bfloat16)  14.3 us
    cos x1, other arithmetic, fourier_basis(): basis = jnp.stack([jnp.cos(angles), -jnp.sin(angles)], axis=2)  13.1 us
    convert_element_type x2, local copies, waits for them, and re-layouts, body(): analysis_table = (basis * (1.0 / math.sqrt(points))).astype(jnp.bfloat16)  12.5 us
  transfers between devices with their start and end apart: 2, of which 2 were waited for; matrix products, arithmetic and copies ran while one was open for 10% of the time, Pallas kernels for 0%

commit v1 on v0

v1 whole, which is shorter than its diff:
```python
import math

import jax
import jax.numpy as jnp
from jax import lax
from jax.experimental import pallas as pl
from jax.experimental.pallas import tpu as pltpu
from jax.sharding import PartitionSpec as P

N = 512
LON = 1536
BF = jnp.bfloat16
F32 = jnp.float32
MESH = pl.DeviceIdType.MESH
NT = (((1,), (1,)), ((), ()))
TN = (((0,), (0,)), ((), ()))


def dot(a, b, dims=(((1,), (0,)), ((), ()))):
    return lax.dot_general(a, b, dims, preferred_element_type=F32)


def cosine(phase):
    w = (jnp.abs(phase - 0.5 * LON) - 0.25 * LON) * (2.0 * math.pi / LON)
    s = w * w
    p = -2.3889859e-08
    for c in (2.7525562e-06, -0.00019840874, 0.0083333310, -0.16666667):
        p = p * s + c
    return w + w * s * p


def wrap(phase):
    return phase - LON * jnp.floor(phase * (1.0 / LON))


def iota(shape, dim):
    return lax.broadcasted_iota(jnp.int32, shape, dim)


def build_table(pairs_row, scale, table, rows=64):
    pairs = table.shape[0] // 4
    spread = jnp.broadcast_to(pairs_row, (128, pairs)).astype(BF)

    @pl.loop(0, table.shape[0] // rows)
    def _(block):
        start = pl.multiple_of(block * rows, rows)
        pick = (start + iota((rows, pairs), 0)) // 4 == iota((rows, pairs), 1)
        lower = dot(pick.astype(F32).astype(BF), spread, NT)
        row = start + iota((rows, 128), 0)
        wave = jnp.where(row // 2 % 2 == 0, lower, N - 1.0 - lower)
        first = wave * iota((rows, 128), 1).astype(F32) + (row % 2).astype(F32) * (LON / 4)
        step = wave * 128.0
        now = cosine(wrap(first)) * scale
        later = cosine(wrap(first + step)) * scale
        twice = 2.0 * cosine(wrap(step))
        for a in range(LON // 128):
            table[pl.ds(start, rows), a * 128:(a + 1) * 128] = now.astype(BF)
            now, later = later, twice * later - now


def kernel(lats, levs, grid, wind, leg, vert, pairs_row, dm_row, pairs_s, out,
           table, wide, ls, lr, zs, zr, ys, yr, ks, kr, merged,
           ls_s, lr_s, zs_s, zr_s, ys_s, yr_s, ks_s, kr_s):
    me_lat, me_lev = lax.axis_index("lat"), lax.axis_index("lev")
    band = grid.shape[0] // 2
    chunks = zs.shape[0]
    barrier = pltpu.get_barrier_semaphore()

    @pl.loop(1, levs)
    def _(d):
        pl.semaphore_signal(barrier, inc=1, device_id={"lev": lax.rem(me_lev + d, levs)}, device_id_type=MESH)

    @pl.loop(1, lats)
    def _(d):
        pl.semaphore_signal(barrier, inc=1, device_id={"lat": lax.rem(me_lat + d, lats)}, device_id_type=MESH)

    build_table(pairs_row[...], 1.0 / math.sqrt(LON), table)
    low = iota((band, 128), 1) < 64
    for p in range(lats // 2):
        both = dot(grid[...], table[p * 128:(p + 1) * 128, :], NT)
        a, b = both[:band], both[band:]
        ls[2 * p] = jnp.where(low, a, pltpu.roll(b, 64, 1)).astype(BF)
        ls[2 * p + 1] = jnp.where(low, pltpu.roll(a, 64, 1), b).astype(BF)

    pl.semaphore_wait(barrier, levs + lats - 2)

    def lat_copy(src, dst, send, recv, t):
        return pltpu.make_async_remote_copy(src, dst, send, recv, device_id={"lat": t}, device_id_type=MESH)

    def lev_copy(src, dst, send, recv, t):
        return pltpu.make_async_remote_copy(src, dst, send, recv, device_id={"lev": t}, device_id_type=MESH)

    def lat_phase(src, dst, send, recv):
        @pl.loop(1, lats)
        def _(d):
            t = lax.rem(me_lat + d, lats)
            lat_copy(src.at[t], dst.at[me_lat], send, recv, t).start()
        dst[me_lat] = src[me_lat]

    def lat_wait(src, dst, send, recv):
        whole = lat_copy(src.at[pl.ds(0, lats - 1)], dst.at[pl.ds(0, lats - 1)], send, recv, me_lat)
        whole.wait_recv()
        whole.wait_send()

    def lev_phase(src, dst, send, recv):
        chips = levs // 2
        @pl.loop(0, levs)
        def _(s):
            k = chips - 1 - s // 2
            h = (k + 1) // 2
            dz = jnp.where(k % 2 == 1, h, chips - h)
            t = lax.rem(me_lev // 2 + dz, chips) * 2 + lax.rem(me_lev + s, 2)

            @pl.when(t != me_lev)
            def _():
                lev_copy(src.at[:, t], dst.at[:, me_lev], send, recv, t).start()
        for q in range(chunks):
            dst[q, me_lev] = src[q, me_lev]

    def lev_wait(src, dst, send, recv):
        whole = lev_copy(src.at[:, pl.ds(0, levs - 1)], dst.at[:, pl.ds(0, levs - 1)], send, recv, me_lev)
        whole.wait_recv()
        whole.wait_send()

    lat_phase(ls, lr, ls_s, lr_s)
    r, s = iota((128, 128), 0), iota((128, 128), 1)
    swap = (s == r % 2 * 64 + r // 2).astype(F32).astype(BF)
    lat_wait(ls, lr, ls_s, lr_s)

    turned = dot(swap, lr[...].reshape(lats * band, 128), NT)
    for q in range(chunks):
        zs[q] = turned[:, q * 128:(q + 1) * 128].astype(BF).reshape(64, 2, 128)
    lev_phase(zs, zr, zs_s, zr_s)

    build_table(pairs_row[...], 1.0 / math.sqrt(N), wide)
    rows = leg.shape[0]
    column = me_lat * levs + me_lev
    lower = pairs_s[column // 4]
    row = iota((rows, 1), 0)
    first = column // 2 % 2 == 0
    bound = N - lower
    own = jnp.where(first, (row < bound).astype(F32), ((row >= bound) & (row <= N)).astype(F32))
    degree = jnp.where(row < bound, lower + row, row - 1)
    degree = jnp.clip(degree, 0, N - 1)
    hit = degree == iota((rows, N), 1)
    index = jnp.sum(jnp.where(hit, dm_row[...].astype(F32), 0.0), axis=1, keepdims=True)
    lev_wait(zs, zr, zs_s, zr_s)

    field = jnp.concatenate([zr[q].reshape(128, 128) for q in range(chunks)], axis=1)
    spectral = dot(leg[...], field, NT) * own
    for op in range(vert.shape[0] // 128):
        merged[:, op * 128:(op + 1) * 128] = jnp.where(index == float(op), spectral, 0.0).astype(BF)
    solved = dot(merged[...], vert[...]).astype(BF)
    coeffs = dot(solved, leg[...], TN)
    for q in range(chunks):
        ys[q] = coeffs[:, q * 128:(q + 1) * 128].astype(BF).reshape(64, 2, 128)
    lev_phase(ys, yr, ys_s, yr_s)
    lev_wait(ys, yr, ys_s, yr_s)

    back = jnp.concatenate(
        [dot(yr[q].reshape(128, 128), swap, TN).astype(BF) for q in range(chunks)], axis=0)
    ks[...] = back.reshape(lats, band, 128)
    lat_phase(ks, kr, ks_s, kr_s)
    lat_wait(ks, kr, ks_s, kr_s)

    tops, ends = [], []
    for p in range(lats // 2):
        a, b = kr[2 * p].astype(F32), kr[2 * p + 1].astype(F32)
        tops.append(jnp.where(low, a, pltpu.roll(b, 64, 1)).astype(BF))
        ends.append(jnp.where(low, pltpu.roll(a, 64, 1), b).astype(BF))
    columns = jnp.concatenate([jnp.concatenate(tops, axis=1), jnp.concatenate(ends, axis=1)], axis=0)
    for x in range(LON // 256):
        cut = slice(x * 256, (x + 1) * 256)
        out[:, cut] = (dot(columns, wide[:, cut]) * wind[:, cut].astype(F32)).astype(BF)


def solution(mesh):
    lats, levs = mesh.shape["lat"], mesh.shape["lev"]

    def body(adjoint_grid, wind, legendre, vertical, pair_table, degree_matrix):
        levels, band, points = adjoint_grid.shape
        rows = legendre.shape[2]
        chunks = legendre.shape[1] // 128
        vmem = pl.BlockSpec(memory_space=pltpu.VMEM)
        smem = pl.BlockSpec(memory_space=pltpu.SMEM)
        lat_block = pltpu.VMEM((lats, band, 128), BF)
        lev_block = pltpu.VMEM((chunks, levs, 2, 128), BF)
        out = pl.pallas_call(
            lambda *refs: kernel(lats, levs, *refs),
            out_shape=jax.ShapeDtypeStruct((levels * band, points), BF),
            in_specs=[vmem] * 6 + [smem],
            out_specs=vmem,
            scratch_shapes=[pltpu.VMEM((4 * pair_table.shape[0], points), BF)] * 2
            + [lat_block] * 2 + [lev_block] * 4 + [lat_block] * 2
            + [pltpu.VMEM((rows, vertical.shape[0] * vertical.shape[1]), BF)]
            + [pltpu.SemaphoreType.DMA] * 8,
            compiler_params=pltpu.CompilerParams(
                collective_id=0, has_side_effects=True, vmem_limit_bytes=60 << 20),
            name="adjoint_step",
        )(
            adjoint_grid.reshape(levels * band, points),
            wind.reshape(levels * band, points),
            jnp.swapaxes(legendre, 1, 2).reshape(rows, legendre.shape[1]),
            vertical.reshape(-1, vertical.shape[2]),
            pair_table.reshape(1, -1),
            degree_matrix.reshape(1, -1),
            pair_table,
        )
        return out.reshape(levels, band, points)

    placed = (
        P("lev", "lat", None),
        P("lev", "lat", None),
        P(("lat", "lev"), None, None),
        P(),
        P(),
        P(),
    )
    return jax.shard_map(
        body, mesh=mesh, in_specs=placed, out_specs=P("lev", "lat", None), check_vma=False
    )
```

time: 199 us -> 90 us (0.45)
  Pallas kernels: 0 us -> 88.1 us
  waiting for transfers between devices: 53.6 us -> 0 us
  starting transfers between devices: 38.1 us -> 0 us
  local copies, waits for them, and re-layouts: 38.2 us -> 1.69 us
  blocking collectives: 24.5 us -> 0 us
  matrix products: 22.5 us -> 0 us
  other arithmetic: 19.1 us -> 0 us
    pallas_call x0 -> x1, Pallas kernels: none -> 88.1 us  [body(): pl.pallas_call(lambda *refs: kernel(lats, levs, *refs), out_shape=jax.Sha...]
    all_to_all x2 -> x0, waiting for transfers between devices: 53.6 us -> none  [the longest x1 31 us: body(): lax.all_to_all(lax.all_to_all(fourier, 'lat', split_axis=0, concat_axis=4...]
    all_to_all x2 -> x0, starting transfers between devices: 38.1 us -> none  [the longest x1 31 us: body(): lax.all_to_all(lax.all_to_all(fourier, 'lat', split_axis=0, concat_axis=4...]
    convert_element_type x4 -> x0, local copies, waits for them, and re-layouts: 26.8 us -> none  [the longest x2 14.3 us: body(): synthesis_table = (basis * (1.0 / math.sqrt(N))).astype(jnp.bfloat16)]
    all_to_all x2 -> x0, blocking collectives: 24.5 us -> none  [the longest x1 14.6 us: body(): lax.all_to_all(fourier, 'lat', split_axis=0, concat_axis=4, tiled=True)]
    dot_general x20 -> x0, matrix products: 22.5 us -> none  [the longest x16 15.5 us: add_matrix(): jnp.einsum('xjm,mg->xjg', spectral_state, vertical[operator_index], prefe...]
    cos x1 -> x0, other arithmetic: 13.1 us -> none  [fourier_basis(): basis = jnp.stack([jnp.cos(angles), -jnp.sin(angles)], axis=2)]
    gather x2 -> x0, local copies, waits for them, and re-layouts: 4.62 us -> none  [the longest x1 3.96 us: body(): matrix_index = jnp.take(degree_matrix, degree)]
  transfers between devices with their start and end apart: 2 -> 0, of which waited for: 2 -> 0; matrix products, arithmetic and copies ran while one was open for 10% -> 0% of each run, Pallas kernels for 0% -> 0%
where the time goes in v1:
time: 90 us; the launch traced here: 89.8 us
  Pallas kernels  88.1 us (98%)
  local copies, waits for them, and re-layouts  1.69 us (2%)
    pallas_call x1, Pallas kernels, body(): pl.pallas_call(lambda *refs: kernel(lats, levs, *refs), out_shape=jax.Sha...  88.1 us

profile of v1, /device:TPU:1, one launch (start us, length us, event | category | flops | bytes accessed | tf_op | source)
XLA Modules:
  0.0 89.8 jit_solution(16414099687761042736)
XLA Ops:
  0.0 88.1 %adjoint_step.1 = bf16[96,1536]{1,0:T(8,128)(2,1)} custom-call(bf16[96,1536]{1,0:T(8,128)(2,1)} %bitcast.12, bf16[96,1536]{1,0:T(8,128)(2,1)} %bitcast.13, bf16[576,768]{1,0:T(8,128)(2,1)} %bitcast.10, bf16[2048,128]{1,0:T(8,128)(2,1)} %bitcast.11, s32[1,256]{1,0:T(1,128)} %bitcast.14, s32[1,512]{1,0:T(1,128)} %bitcast.15, s32[256]{0:T(256)} %refs_6_.1), custom_call_target="tpu_custom_call" | custom-call | tf_op jit(solution)/shard_map/adjoint_step/pallas_call | solution.py:188
  88.1 1.7 %copy.8 = bf16[2,48,1536]{2,1,0:T(8,128)(2,1)} copy(bf16[2,48,1536]{2,1,0:T(8,128)(2,1)} %bitcast.9) | data formatting | bytes 589824

commit v2 on v1

--- a/solution.py
+++ b/solution.py
@@ -58,21 +58,32 @@
             now, later = later, twice * later - now
 
 
-def kernel(lats, levs, grid, wind, leg, vert, pairs_row, dm_row, pairs_s, out,
-           table, wide, ls, lr, zs, zr, ys, yr, ks, kr, merged,
-           ls_s, lr_s, zs_s, zr_s, ys_s, yr_s, ks_s, kr_s):
+def kernel(lats, levs, grid, wind_h, leg_h, vert_h, pairs_row, dm_row, pairs_s, out,
+           wind, leg, vert, table, wide, ls, lr, zs, zr, ys, yr, ks, kr, merged,
+           ls_s, lr_s, zs_s, zr_s, ys_s, yr_s, ks_s, kr_s, load_s, plane_s, line_s):
     me_lat, me_lev = lax.axis_index("lat"), lax.axis_index("lev")
     band = grid.shape[0] // 2
     chunks = zs.shape[0]
+    chips = levs // 2
+    me_z, core = me_lev // 2, lax.rem(me_lev, 2)
+    loads = [pltpu.make_async_copy(src, dst, load_s.at[n])
+             for n, (src, dst) in enumerate(((leg_h, leg), (vert_h, vert), (wind_h, wind)))]
+    for load in loads:
+        load.start()
+
     barrier = pltpu.get_barrier_semaphore()
 
-    @pl.loop(1, levs)
+    @pl.loop(1, chips)
     def _(d):
-        pl.semaphore_signal(barrier, inc=1, device_id={"lev": lax.rem(me_lev + d, levs)}, device_id_type=MESH)
+        pl.semaphore_signal(barrier, inc=1, device_id={"lev": lax.rem(me_z + d, chips) * 2}, device_id_type=MESH)
 
     @pl.loop(1, lats)
     def _(d):
-        pl.semaphore_signal(barrier, inc=1, device_id={"lat": lax.rem(me_lat + d, lats)}, device_id_type=MESH)
+        pl.semaphore_signal(barrier, inc=1, device_id=(lax.rem(me_lat + d, lats), me_z * 2 + 1), device_id_type=MESH)
+
+    @pl.when(core == 0)
+    def _():
+        pl.semaphore_signal(barrier, inc=1, device_id={"lev": me_lev + 1}, device_id_type=MESH)
 
     build_table(pairs_row[...], 1.0 / math.sqrt(LON), table)
     low = iota((band, 128), 1) < 64
@@ -82,7 +93,14 @@
         ls[2 * p] = jnp.where(low, a, pltpu.roll(b, 64, 1)).astype(BF)
         ls[2 * p + 1] = jnp.where(low, pltpu.roll(a, 64, 1), b).astype(BF)
 
-    pl.semaphore_wait(barrier, levs + lats - 2)
+    @pl.when(core == 1)
+    def _():
+        pl.semaphore_wait(barrier, 2 * lats - 1)
+        pl.semaphore_signal(plane_s, inc=1, device_id={"lev": me_lev - 1}, device_id_type=MESH)
+
+    @pl.when(core == 0)
+    def _():
+        pl.semaphore_wait(plane_s, 1)
 
     def lat_copy(src, dst, send, recv, t):
         return pltpu.make_async_remote_copy(src, dst, send, recv, device_id={"lat": t}, device_id_type=MESH)
@@ -102,14 +120,13 @@
         whole.wait_recv()
         whole.wait_send()
 
-    def lev_phase(src, dst, send, recv):
-        chips = levs // 2
+    def lev_phase(src, dst, send, recv, waves):
         @pl.loop(0, levs)
         def _(s):
-            k = chips - 1 - s // 2
+            k = chips - 1 - lax.rem(s, chips) if waves else chips - 1 - s // 2
             h = (k + 1) // 2
             dz = jnp.where(k % 2 == 1, h, chips - h)
-            t = lax.rem(me_lev // 2 + dz, chips) * 2 + lax.rem(me_lev + s, 2)
+            t = lax.rem(me_z + dz, chips) * 2 + (s // chips if waves else lax.rem(me_lev + s, 2))
 
             @pl.when(t != me_lev)
             def _():
@@ -130,7 +147,17 @@
     turned = dot(swap, lr[...].reshape(lats * band, 128), NT)
     for q in range(chunks):
         zs[q] = turned[:, q * 128:(q + 1) * 128].astype(BF).reshape(64, 2, 128)
-    lev_phase(zs, zr, zs_s, zr_s)
+
+    @pl.when(core == 0)
+    def _():
+        pl.semaphore_wait(barrier, levs - 2)
+        pl.semaphore_signal(line_s, inc=1, device_id={"lev": me_lev + 1}, device_id_type=MESH)
+
+    @pl.when(core == 1)
+    def _():
+        pl.semaphore_wait(line_s, 1)
+
+    lev_phase(zs, zr, zs_s, zr_s, True)
 
     build_table(pairs_row[...], 1.0 / math.sqrt(N), wide)
     rows = leg.shape[0]
@@ -144,6 +171,8 @@
     degree = jnp.clip(degree, 0, N - 1)
     hit = degree == iota((rows, N), 1)
     index = jnp.sum(jnp.where(hit, dm_row[...].astype(F32), 0.0), axis=1, keepdims=True)
+    for load in loads:
+        load.wait()
     lev_wait(zs, zr, zs_s, zr_s)
 
     field = jnp.concatenate([zr[q].reshape(128, 128) for q in range(chunks)], axis=1)
@@ -154,7 +183,7 @@
     coeffs = dot(solved, leg[...], TN)
     for q in range(chunks):
         ys[q] = coeffs[:, q * 128:(q + 1) * 128].astype(BF).reshape(64, 2, 128)
-    lev_phase(ys, yr, ys_s, yr_s)
+    lev_phase(ys, yr, ys_s, yr_s, False)
     lev_wait(ys, yr, ys_s, yr_s)
 
     back = jnp.concatenate(
@@ -188,12 +217,18 @@
         out = pl.pallas_call(
             lambda *refs: kernel(lats, levs, *refs),
             out_shape=jax.ShapeDtypeStruct((levels * band, points), BF),
-            in_specs=[vmem] * 6 + [smem],
+            in_specs=[vmem] + [pl.BlockSpec(memory_space=pl.ANY)] * 3 + [vmem] * 2 + [smem],
             out_specs=vmem,
-            scratch_shapes=[pltpu.VMEM((4 * pair_table.shape[0], points), BF)] * 2
+            scratch_shapes=[
+                pltpu.VMEM((levels * band, points), BF),
+                pltpu.VMEM((rows, legendre.shape[1]), BF),
+                pltpu.VMEM((vertical.shape[0] * vertical.shape[1], vertical.shape[2]), BF),
+            ]
+            + [pltpu.VMEM((4 * pair_table.shape[0], points), BF)] * 2
             + [lat_block] * 2 + [lev_block] * 4 + [lat_block] * 2
             + [pltpu.VMEM((rows, vertical.shape[0] * vertical.shape[1]), BF)]
-            + [pltpu.SemaphoreType.DMA] * 8,
+            + [pltpu.SemaphoreType.DMA] * 8
+            + [pltpu.SemaphoreType.DMA((3,)), pltpu.SemaphoreType.REGULAR, pltpu.SemaphoreType.REGULAR],
             compiler_params=pltpu.CompilerParams(
                 collective_id=0, has_side_effects=True, vmem_limit_bytes=60 << 20),
             name="adjoint_step",

time: 90 us -> 82.1 us (0.912)
  Pallas kernels: 88.1 us -> 80.2 us
    pallas_call x1, Pallas kernels: 88.1 us -> 80.2 us  [body(): pl.pallas_call(lambda *refs: kernel(lats, levs, *refs), out_shape=jax.Sha...]
where the time goes in v2:
time: 82.1 us; the launch traced here: 81.9 us
  Pallas kernels  80.2 us (98%)
  local copies, waits for them, and re-layouts  1.69 us (2%)
    pallas_call x1, Pallas kernels, body(): pl.pallas_call(lambda *refs: kernel(lats, levs, *refs), out_shape=jax.Sha...  80.2 us
    unnamed x1, local copies, waits for them, and re-layouts  1.69 us

profile of v2, /device:TPU:1, one launch (start us, length us, event | category | flops | bytes accessed | tf_op | source)
XLA Modules:
  0.0 81.9 jit_solution(3104631259146993427)
XLA Ops:
  0.0 80.2 %adjoint_step.1 = bf16[96,1536]{1,0:T(8,128)(2,1)} custom-call(bf16[96,1536]{1,0:T(8,128)(2,1)} %bitcast.12, bf16[96,1536]{1,0:T(8,128)(2,1)} %bitcast.13, bf16[576,768]{1,0:T(8,128)(2,1)} %bitcast.10, bf16[2048,128]{1,0:T(8,128)(2,1)} %bitcast.11, s32[1,256]{1,0:T(1,128)} %bitcast.14, s32[1,512]{1,0:T(1,128)} %bitcast.15, s32[256]{0:T(256)} %refs_6_.1), custom_call_target="tpu_custom_call" | custom-call | tf_op jit(solution)/shard_map/adjoint_step/pallas_call | solution.py:217
  80.2 1.7 %copy.8 = bf16[2,48,1536]{2,1,0:T(8,128)(2,1)} copy(bf16[2,48,1536]{2,1,0:T(8,128)(2,1)} %bitcast.9) | data formatting | bytes 589824

commit v3 on v2

--- a/solution.py
+++ b/solution.py
@@ -37,45 +37,50 @@
     return lax.broadcasted_iota(jnp.int32, shape, dim)
 
 
-def build_table(pairs_row, scale, table, rows=64):
-    pairs = table.shape[0] // 4
+def waves_of(pairs_row, waves):
+    rows, pairs = waves.shape[0], pairs_row.shape[1]
     spread = jnp.broadcast_to(pairs_row, (128, pairs)).astype(BF)
-
-    @pl.loop(0, table.shape[0] // rows)
-    def _(block):
-        start = pl.multiple_of(block * rows, rows)
-        pick = (start + iota((rows, pairs), 0)) // 4 == iota((rows, pairs), 1)
-        lower = dot(pick.astype(F32).astype(BF), spread, NT)
-        row = start + iota((rows, 128), 0)
-        wave = jnp.where(row // 2 % 2 == 0, lower, N - 1.0 - lower)
-        first = wave * iota((rows, 128), 1).astype(F32) + (row % 2).astype(F32) * (LON / 4)
-        step = wave * 128.0
-        now = cosine(wrap(first)) * scale
-        later = cosine(wrap(first + step)) * scale
-        twice = 2.0 * cosine(wrap(step))
-        for a in range(LON // 128):
-            table[pl.ds(start, rows), a * 128:(a + 1) * 128] = now.astype(BF)
-            now, later = later, twice * later - now
-
-
-def kernel(lats, levs, grid, wind_h, leg_h, vert_h, pairs_row, dm_row, pairs_s, out,
-           wind, leg, vert, table, wide, ls, lr, zs, zr, ys, yr, ks, kr, merged,
+    pick = iota((rows, pairs), 0) // 4 == iota((rows, pairs), 1)
+    lower = dot(pick.astype(F32).astype(BF), spread, NT)
+    waves[...] = jnp.where(iota((rows, 128), 0) // 2 % 2 == 0, lower, N - 1.0 - lower)
+
+
+def table_rows(waves, scale, table, start, rows):
+    wave = waves[pl.ds(start, rows), :]
+    quarter = (iota((rows, 128), 0) % 2).astype(F32) * (LON / 4)
+    first = wave * iota((rows, 128), 1).astype(F32) + quarter
+    step = wave * 128.0
+    now = cosine(wrap(first)) * scale
+    later = cosine(wrap(first + step)) * scale
+    twice = 2.0 * cosine(wrap(step))
+    sign = 1.0 - 2.0 * (wave - 2.0 * jnp.floor(wave * 0.5))
+    half = LON // 256
+    for a in range(half):
+        table[pl.ds(start, rows), a * 128:(a + 1) * 128] = now.astype(BF)
+        table[pl.ds(start, rows), (half + a) * 128:(half + a + 1) * 128] = (now * sign).astype(BF)
+        now, later = later, twice * later - now
+
+
+def kernel(lats, levs, grid_h, wind_h, leg_h, vert_h, pairs_h, dm_h, flat_h,
+           columns, wide, wind, pairs_row, dm_row, pairs_s, grid, leg, vert, table, waves, ls, lr, zs, zr, ys, yr, ks, kr, merged, masks, paired,
            ls_s, lr_s, zs_s, zr_s, ys_s, yr_s, ks_s, kr_s, load_s, plane_s, line_s):
     me_lat, me_lev = lax.axis_index("lat"), lax.axis_index("lev")
-    band = grid.shape[0] // 2
+    band = grid_h.shape[0] // 2
     chunks = zs.shape[0]
     chips = levs // 2
     me_z, core = me_lev // 2, lax.rem(me_lev, 2)
     loads = [pltpu.make_async_copy(src, dst, load_s.at[n])
-             for n, (src, dst) in enumerate(((leg_h, leg), (vert_h, vert), (wind_h, wind)))]
-    for load in loads:
-        load.start()
+             for n, (src, dst) in enumerate((
+                 (pairs_h, pairs_row), (grid_h, grid), (flat_h, pairs_s), (dm_h, dm_row),
+                 (leg_h, leg), (vert_h, vert), (wind_h, wind)))]
 
     barrier = pltpu.get_barrier_semaphore()
 
-    @pl.loop(1, chips)
-    def _(d):
-        pl.semaphore_signal(barrier, inc=1, device_id={"lev": lax.rem(me_z + d, chips) * 2}, device_id_type=MESH)
+    @pl.loop(0, chips - 1)
+    def _(k):
+        h = (chips - k) // 2
+        z = lax.rem(me_z + jnp.where(lax.rem(k, 2) == 0, h, chips - h), chips)
+        pl.semaphore_signal(barrier, inc=1, device_id={"lev": z * 2}, device_id_type=MESH)
 
     @pl.loop(1, lats)
     def _(d):
@@ -85,14 +90,25 @@
     def _():
         pl.semaphore_signal(barrier, inc=1, device_id={"lev": me_lev + 1}, device_id_type=MESH)
 
-    build_table(pairs_row[...], 1.0 / math.sqrt(LON), table)
+    for load in loads:
+        load.start()
+    loads[0].wait()
+    waves_of(pairs_row[...], waves)
     low = iota((band, 128), 1) < 64
-    for p in range(lats // 2):
+
+    def transform(p):
         both = dot(grid[...], table[p * 128:(p + 1) * 128, :], NT)
         a, b = both[:band], both[band:]
         ls[2 * p] = jnp.where(low, a, pltpu.roll(b, 64, 1)).astype(BF)
         ls[2 * p + 1] = jnp.where(low, pltpu.roll(a, 64, 1), b).astype(BF)
 
+    loads[1].wait()
+    for p in range(lats // 2):
+        table_rows(waves, 1.0 / math.sqrt(LON), table, p * 128, 128)
+        if p > 0:
+            transform(p - 1)
+    transform(lats // 2 - 1)
+
     @pl.when(core == 1)
     def _():
         pl.semaphore_wait(barrier, 2 * lats - 1)
@@ -109,9 +125,11 @@
         return pltpu.make_async_remote_copy(src, dst, send, recv, device_id={"lev": t}, device_id_type=MESH)
 
     def lat_phase(src, dst, send, recv):
-        @pl.loop(1, lats)
-        def _(d):
-            t = lax.rem(me_lat + d, lats)
+        width = math.isqrt(lats)
+        steps = [(dy, dx) for dy in range(width) for dx in range(width) if dy or dx]
+        steps.sort(key=lambda step: -sum(min(d, width - d) for d in step))
+        for dy, dx in steps:
+            t = lax.rem(me_lat // width + dy, width) * width + lax.rem(me_lat + dx, width)
             lat_copy(src.at[t], dst.at[me_lat], send, recv, t).start()
         dst[me_lat] = src[me_lat]
 
@@ -159,9 +177,14 @@
 
     lev_phase(zs, zr, zs_s, zr_s, True)
 
-    build_table(pairs_row[...], 1.0 / math.sqrt(N), wide)
-    rows = leg.shape[0]
+    @pl.loop(0, wide.shape[0] // 128)
+    def _(block):
+        table_rows(waves, 1.0 / math.sqrt(N), wide, pl.multiple_of(block * 128, 128), 128)
+
+    rows = leg_h.shape[0]
     column = me_lat * levs + me_lev
+    for load in loads[2:]:
+        load.wait()
     lower = pairs_s[column // 4]
     row = iota((rows, 1), 0)
     first = column // 2 % 2 == 0
@@ -171,15 +194,22 @@
     degree = jnp.clip(degree, 0, N - 1)
     hit = degree == iota((rows, N), 1)
     index = jnp.sum(jnp.where(hit, dm_row[...].astype(F32), 0.0), axis=1, keepdims=True)
-    for load in loads:
-        load.wait()
+    slots = vert_h.shape[0] // 256
+    slot = jnp.floor(index * 0.5)
+    for n in range(slots):
+        chosen = jnp.where(slot == float(n), own, 0.0)
+        masks[:, n * 128:(n + 1) * 128] = jnp.broadcast_to(chosen, (rows, 128)).astype(BF)
+        for h in range(2):
+            paired[n * 128:(n + 1) * 128, h * 128:(h + 1) * 128] = vert[(2 * n + h) * 128:(2 * n + h + 1) * 128, :]
     lev_wait(zs, zr, zs_s, zr_s)
 
     field = jnp.concatenate([zr[q].reshape(128, 128) for q in range(chunks)], axis=1)
-    spectral = dot(leg[...], field, NT) * own
-    for op in range(vert.shape[0] // 128):
-        merged[:, op * 128:(op + 1) * 128] = jnp.where(index == float(op), spectral, 0.0).astype(BF)
-    solved = dot(merged[...], vert[...]).astype(BF)
+    spectral = dot(leg[...], field, NT).astype(BF)
+    for n in range(slots):
+        cut = slice(n * 128, (n + 1) * 128)
+        merged[:, cut] = spectral * masks[:, cut]
+    both = dot(merged[...], paired[...])
+    solved = jnp.where(index == 2.0 * slot, both[:, :128], both[:, 128:]).astype(BF)
     coeffs = dot(solved, leg[...], TN)
     for q in range(chunks):
         ys[q] = coeffs[:, q * 128:(q + 1) * 128].astype(BF).reshape(64, 2, 128)
@@ -197,10 +227,13 @@
         a, b = kr[2 * p].astype(F32), kr[2 * p + 1].astype(F32)
         tops.append(jnp.where(low, a, pltpu.roll(b, 64, 1)).astype(BF))
         ends.append(jnp.where(low, pltpu.roll(a, 64, 1), b).astype(BF))
-    columns = jnp.concatenate([jnp.concatenate(tops, axis=1), jnp.concatenate(ends, axis=1)], axis=0)
+    columns[...] = jnp.concatenate([jnp.concatenate(tops, axis=1), jnp.concatenate(ends, axis=1)], axis=0)
+
+
+def synthesis(columns, wide, wind, out):
     for x in range(LON // 256):
         cut = slice(x * 256, (x + 1) * 256)
-        out[:, cut] = (dot(columns, wide[:, cut]) * wind[:, cut].astype(F32)).astype(BF)
+        out[:, cut] = (dot(columns[...], wide[:, cut]) * wind[:, cut].astype(F32)).astype(BF)
 
 
 def solution(mesh):
@@ -211,28 +244,36 @@
         rows = legendre.shape[2]
         chunks = legendre.shape[1] // 128
         vmem = pl.BlockSpec(memory_space=pltpu.VMEM)
-        smem = pl.BlockSpec(memory_space=pltpu.SMEM)
         lat_block = pltpu.VMEM((lats, band, 128), BF)
         lev_block = pltpu.VMEM((chunks, levs, 2, 128), BF)
-        out = pl.pallas_call(
+        parts = pl.pallas_call(
             lambda *refs: kernel(lats, levs, *refs),
-            out_shape=jax.ShapeDtypeStruct((levels * band, points), BF),
-            in_specs=[vmem] + [pl.BlockSpec(memory_space=pl.ANY)] * 3 + [vmem] * 2 + [smem],
-            out_specs=vmem,
+            out_shape=[
+                jax.ShapeDtypeStruct((levels * band, 4 * pair_table.shape[0]), BF),
+                jax.ShapeDtypeStruct((4 * pair_table.shape[0], points), BF),
+                jax.ShapeDtypeStruct((levels * band, points), BF),
+            ],
+            in_specs=[pl.BlockSpec(memory_space=pl.ANY)] * 7,
+            out_specs=[vmem] * 3,
             scratch_shapes=[
+                pltpu.VMEM((1, pair_table.shape[0]), jnp.int32),
+                pltpu.VMEM((1, degree_matrix.shape[0]), jnp.int32),
+                pltpu.SMEM(pair_table.shape, jnp.int32),
                 pltpu.VMEM((levels * band, points), BF),
                 pltpu.VMEM((rows, legendre.shape[1]), BF),
                 pltpu.VMEM((vertical.shape[0] * vertical.shape[1], vertical.shape[2]), BF),
             ]
-            + [pltpu.VMEM((4 * pair_table.shape[0], points), BF)] * 2
+            + [pltpu.VMEM((4 * pair_table.shape[0], points), BF)]
+            + [pltpu.VMEM((4 * pair_table.shape[0], 128), F32)]
             + [lat_block] * 2 + [lev_block] * 4 + [lat_block] * 2
-            + [pltpu.VMEM((rows, vertical.shape[0] * vertical.shape[1]), BF)]
+            + [pltpu.VMEM((rows, vertical.shape[0] // 2 * vertical.shape[1]), BF)] * 2
+            + [pltpu.VMEM((vertical.shape[0] // 2 * vertical.shape[1], 2 * vertical.shape[2]), BF)]
             + [pltpu.SemaphoreType.DMA] * 8
-            + [pltpu.SemaphoreType.DMA((3,)), pltpu.SemaphoreType.REGULAR, pltpu.SemaphoreType.REGULAR],
+            + [pltpu.SemaphoreType.DMA((7,)), pltpu.SemaphoreType.REGULAR, pltpu.SemaphoreType.REGULAR],
             compiler_params=pltpu.CompilerParams(
-                collective_id=0, has_side_effects=True, vmem_limit_bytes=60 << 20),
+                collective_id=0, has_side_effects=True, vmem_limit_bytes=32 << 20),
             name="adjoint_step",
-        )(
+        )(*[pltpu.with_memory_space_constraint(array, pltpu.HBM) for array in (
             adjoint_grid.reshape(levels * band, points),
             wind.reshape(levels * band, points),
             jnp.swapaxes(legendre, 1, 2).reshape(rows, legendre.shape[1]),
@@ -240,7 +281,15 @@
             pair_table.reshape(1, -1),
             degree_matrix.reshape(1, -1),
             pair_table,
-        )
+        )])
+        out = pl.pallas_call(
+            synthesis,
+            out_shape=jax.ShapeDtypeStruct((levels * band, points), BF),
+            in_specs=[vmem] * 3,
+            out_specs=vmem,
+            compiler_params=pltpu.CompilerParams(vmem_limit_bytes=12 << 20),
+            name="synthesis",
+        )(*parts)
         return out.reshape(levels, band, points)
 
     placed = (

time: 82.1 us -> 78 us (0.950)
  Pallas kernels: 80.2 us -> 77.9 us
  local copies, waits for them, and re-layouts: 1.69 us -> 0 us
    pallas_call x1 -> x2, Pallas kernels: 80.2 us -> 77.9 us  [the longest x1 76.5 us: body(): pl.pallas_call(lambda *refs: kernel(lats, levs, *refs), out_shape=[jax.Sh...]
    unnamed x1 -> x0, local copies, waits for them, and re-layouts: 1.69 us -> none
where the time goes in v3:
time: 78 us; the launch traced here: 77.9 us
  Pallas kernels  77.9 us (100%)
    pallas_call x1, Pallas kernels, body(): pl.pallas_call(lambda *refs: kernel(lats, levs, *refs), out_shape=[jax.Sh...  76.5 us

profile of v3, /device:TPU:1, one launch (start us, length us, event | category | flops | bytes accessed | tf_op | source)
XLA Modules:
  0.0 77.9 jit_solution(507332163701984493)
XLA Ops:
  0.0 76.5 %adjoint_step.1 = (bf16[96,1024]{1,0:T(8,128)(2,1)S(1)}, bf16[1024,1536]{1,0:T(8,128)(2,1)S(1)}, bf16[96,1536]{1,0:T(8,128)(2,1)S(1)}) custom-call(bf16[96,1536]{1,0:T(8,128)(2,1)} %bitcast.11, bf16[96,1536]{1,0:T(8,128)(2,1)} %bitcast.12, bf16[576,768]{1,0:T(8,128)(2,1)} %bitcast.9, bf16[2048,128]{1,0:T(8,128)(2,1)} %bitcast.10, s32[1,256]{1,0:T(1,128)} %bitcast.13, ...), custom_call_target="tpu_custom_call" | custom-call | tf_op jit(solution)/shard_map/adjoint_step/pallas_call | solution.py:249
  76.5 1.3 %synthesis.1 = bf16[96,1536]{1,0:T(8,128)(2,1)} custom-call(bf16[96,1024]{1,0:T(8,128)(2,1)S(1)} %get-tuple-element.8.columns, bf16[1024,1536]{1,0:T(8,128)(2,1)S(1)} %get-tuple-element.9.wide, bf16[96,1536]{1,0:T(8,128)(2,1)S(1)} %get-tuple-element.10.wind), custom_call_target="tpu_custom_call" | custom-call | tf_op jit(solution)/shard_map/synthesis/pallas_call | solution.py:285

commit v4 on v3

--- a/solution.py
+++ b/solution.py
@@ -230,10 +230,16 @@
     columns[...] = jnp.concatenate([jnp.concatenate(tops, axis=1), jnp.concatenate(ends, axis=1)], axis=0)
 
 
-def synthesis(columns, wide, wind, out):
-    for x in range(LON // 256):
-        cut = slice(x * 256, (x + 1) * 256)
-        out[:, cut] = (dot(columns[...], wide[:, cut]) * wind[:, cut].astype(F32)).astype(BF)
+def synthesis(columns, wide, wind, out, part, sems):
+    copies = []
+    width = part.shape[2]
+    for n in range(part.shape[0]):
+        cut = slice(n * width, (n + 1) * width)
+        part[n] = (dot(columns[...], wide[:, cut]) * wind[:, cut].astype(F32)).astype(BF)
+        copies.append(pltpu.make_async_copy(part.at[n], out.at[:, cut], sems.at[n]))
+        copies[-1].start()
+    for copy in copies:
+        copy.wait()
 
 
 def solution(mesh):
@@ -286,7 +292,11 @@
             synthesis,
             out_shape=jax.ShapeDtypeStruct((levels * band, points), BF),
             in_specs=[vmem] * 3,
-            out_specs=vmem,
+            out_specs=pl.BlockSpec(memory_space=pl.ANY),
+            scratch_shapes=[
+                pltpu.VMEM((points // 256, levels * band, 256), BF),
+                pltpu.SemaphoreType.DMA((points // 256,)),
+            ],
             compiler_params=pltpu.CompilerParams(vmem_limit_bytes=12 << 20),
             name="synthesis",
         )(*parts)

time: 78 us -> 78 us (level)
  no operation moved by 1% of the time
where the time goes in v4:
time: 78 us; the launch traced here: 77.8 us
  Pallas kernels  77.8 us (100%)
    pallas_call x1, Pallas kernels, body(): pl.pallas_call(lambda *refs: kernel(lats, levs, *refs), out_shape=[jax.Sh...  76.5 us

profile of v4, /device:TPU:1, one launch (start us, length us, event | category | flops | bytes accessed | tf_op | source)
XLA Modules:
  0.0 77.8 jit_solution(14766328493733297399)
XLA Ops:
  0.0 76.5 %adjoint_step.1 = (bf16[96,1024]{1,0:T(8,128)(2,1)S(1)}, bf16[1024,1536]{1,0:T(8,128)(2,1)S(1)}, bf16[96,1536]{1,0:T(8,128)(2,1)S(1)}) custom-call(bf16[96,1536]{1,0:T(8,128)(2,1)} %bitcast.11, bf16[96,1536]{1,0:T(8,128)(2,1)} %bitcast.12, bf16[576,768]{1,0:T(8,128)(2,1)} %bitcast.9, bf16[2048,128]{1,0:T(8,128)(2,1)} %bitcast.10, s32[1,256]{1,0:T(1,128)} %bitcast.13, ...), custom_call_target="tpu_custom_call" | custom-call | tf_op jit(solution)/shard_map/adjoint_step/pallas_call | solution.py:255
  76.5 1.3 %synthesis.1 = bf16[96,1536]{1,0:T(8,128)(2,1)} custom-call(bf16[96,1024]{1,0:T(8,128)(2,1)S(1)} %get-tuple-element.8.columns, bf16[1024,1536]{1,0:T(8,128)(2,1)S(1)} %get-tuple-element.9.wide, bf16[96,1536]{1,0:T(8,128)(2,1)S(1)} %get-tuple-element.10.wind), custom_call_target="tpu_custom_call" | custom-call | tf_op jit(solution)/shard_map/synthesis/pallas_call | solution.py:291
